TPU v7x, 512 devices: a whole 4x8x8 slice. The times are simulated.
512 devices in a mesh: section: 4 (over x), sub: 32 (over z_lo, y), rng: 4 (over z_hi, core).
Axes of the slice: x: 4, y: 8, z: 8 (z_hi: 2, z_lo: 4; z = z_hi * 4 + z_lo), core: 2. Of those that a mesh axis runs over, the one named last changes fastest.
Arguments:
- echoes: bfloat16 [2, 32, 24, 16384], P(None, 'sub', 'section', 'rng'), may hold values from -6 to 6
- chirp: bfloat16 [2, 2048], replicated, may hold values from -0.25 to 0.25
- steer: bfloat16 [2, 32, 128, 24], P(None, 'sub'), may hold values from -2 to 2
- pulse_order: int32 [32, 24], P('sub'), may hold values from 0 to 23, each once within a row
- band_coef: bfloat16 [5, 32, 2, 2, 128, 16], P(None, 'sub'), may hold values from -2.5 to 2.5
- band_start: int32 [5, 32, 2, 128], P(None, 'sub'), may hold values from 0 to 112
- band_width: int32 [5, 32, 2, 128], P(None, 'sub'), may hold values from 1 to 16
Outputs:
- image: bfloat16 [2, 4096, 4, 4096], P(None, 'sub', 'rng', 'section')
Inputs may be any that keep to these rules, and one draw needn't show every extreme that they name: `pulse_order`: each row is a permutation of the 24 aperture positions.
All inputs are finite; a program needn't handle non-finite values.
Results may differ from a plain program's by a relative error of at most 0.0085.
Values may be sent and summed in bfloat16 or wider, within the bound.
A program may use at most 64 MiB of HBM per device.

v0:
```python
import jax
import jax.numpy as jnp
from jax import lax
from jax.sharding import PartitionSpec as P

CBLK = 128


def from_behind(value, axis, by):
    size = lax.axis_size(axis)
    pairs = [(i, i + by) for i in range(size) if 0 <= i + by < size]
    return lax.ppermute(value, axis, pairs)


def from_partner(block, axis, stride):
    count = lax.axis_size(axis)
    route = []
    for low in range(count):
        high = low | 1 << stride
        if high != low and high < count:
            route += [(low, high), (high, low)]
    return lax.ppermute(block, axis, route)


def band_matrix(coef_side, start_side, width_side):
    beam_count = coef_side.shape[1]
    tap_count = coef_side.shape[2]
    column = jnp.arange(beam_count, dtype=jnp.int32)
    offset = column[None, :] - start_side[:, None]
    taps = jnp.arange(tap_count, dtype=jnp.int32)
    hits = (offset[None, :, :] == taps[:, None, None]) & (
        taps[:, None, None] < width_side[None, :, None]
    )
    selector = hits.astype(jnp.bfloat16)
    return jnp.einsum(
        "sqt,tqc->sqc", coef_side, selector, preferred_element_type=jnp.float32
    ).astype(jnp.bfloat16)


def merge_level(own, partner_image, coef_level, start_level, width_level):
    self_matrix = band_matrix(coef_level[0], start_level[0], width_level[0])
    cross_matrix = band_matrix(coef_level[1], start_level[1], width_level[1])
    upper_rows = jnp.concatenate(
        [self_matrix[0], -self_matrix[1], cross_matrix[0], -cross_matrix[1]], axis=1
    )
    lower_rows = jnp.concatenate(
        [self_matrix[1], self_matrix[0], cross_matrix[1], cross_matrix[0]], axis=1
    )
    operator = jnp.concatenate([upper_rows, lower_rows], axis=0)
    stacked = jnp.concatenate([own[0], own[1], partner_image[0], partner_image[1]], axis=0)
    merged = jnp.dot(operator, stacked, preferred_element_type=jnp.float32)
    return merged.reshape(2, own.shape[1], own.shape[2]).astype(jnp.bfloat16)


def lag_tables(chirp, extra_blocks):
    tap_count = chirp.shape[1]
    padded = jnp.concatenate(
        [jnp.zeros((2, CBLK), jnp.bfloat16), chirp, jnp.zeros((2, 2 * CBLK), jnp.bfloat16)], axis=1
    )
    total_len = tap_count + 3 * CBLK
    tiled = jnp.tile(padded, (1, CBLK))[:, : CBLK * (total_len - 1)]
    shifted = tiled.reshape(2, CBLK, total_len - 1)[:, :, CBLK : CBLK + (extra_blocks + 1) * CBLK]
    shifted = shifted.reshape(2, CBLK, extra_blocks + 1, CBLK)
    return jnp.transpose(shifted, (0, 2, 3, 1))


def compress(signal, chirp):
    pulse_count = signal.shape[1]
    range_count = signal.shape[2]
    tap_count = chirp.shape[1]
    next_rim = from_behind(signal[:, :, :tap_count], "rng", -1)
    extended = jnp.concatenate([signal, next_rim], axis=2)
    block_count = range_count // CBLK
    extra_blocks = tap_count // CBLK
    blocks = extended.reshape(2, pulse_count, block_count + extra_blocks, CBLK)
    blocks = jnp.transpose(blocks, (1, 2, 0, 3)).reshape(
        pulse_count, block_count + extra_blocks, 2 * CBLK
    )
    parts_table = lag_tables(chirp, extra_blocks)
    chirp_real = parts_table[0]
    chirp_imag = parts_table[1]
    upper_rows = jnp.concatenate([chirp_real, -chirp_imag], axis=2)
    lower_rows = jnp.concatenate([chirp_imag, chirp_real], axis=2)
    tables = jnp.concatenate([upper_rows, lower_rows], axis=1)

    def add_piece(lag, accumulated):
        window = lax.dynamic_slice_in_dim(blocks, lag, block_count, 1)
        table = lax.dynamic_index_in_dim(tables, lag, 0, keepdims=False)
        return accumulated + jnp.einsum(
            "pbi,io->pbo", window, table, preferred_element_type=jnp.float32
        )

    accumulated = lax.fori_loop(
        0, extra_blocks + 1, add_piece, jnp.zeros((pulse_count, block_count, 2 * CBLK), jnp.float32)
    )
    accumulated = accumulated.reshape(pulse_count, block_count, 2, CBLK)
    return (
        jnp.transpose(accumulated, (2, 0, 1, 3))
        .reshape(2, pulse_count, range_count)
        .astype(jnp.bfloat16)
    )


def on_device(echoes, chirp, steer, pulse_order, band_coef, band_start, band_width):
    compressed = compress(echoes[:, 0], chirp)
    pulse_rows = lax.all_to_all(compressed, "section", split_axis=2, concat_axis=1, tiled=True)
    position_count = pulse_order.shape[1]
    positions = jnp.arange(position_count, dtype=jnp.int32)
    selector = (positions[:, None] == pulse_order[0][None, :]).astype(jnp.bfloat16)
    weights = jnp.einsum(
        "sqj,jk->sqk", steer[:, 0], selector, preferred_element_type=jnp.float32
    ).astype(jnp.bfloat16)
    forming = jnp.concatenate(
        [
            jnp.concatenate([weights[0], -weights[1]], axis=1),
            jnp.concatenate([weights[1], weights[0]], axis=1),
        ],
        axis=0,
    )
    stacked_rows = jnp.concatenate([pulse_rows[0], pulse_rows[1]], axis=0)
    beam_count = weights.shape[1]
    level_image = (
        jnp.dot(forming, stacked_rows, preferred_element_type=jnp.float32)
        .reshape(2, beam_count, pulse_rows.shape[2])
        .astype(jnp.bfloat16)
    )
    bit_count = lax.axis_size("sub").bit_length() - 1
    coef_all = band_coef[:, 0]
    start_all = band_start[:, 0]
    width_all = band_width[:, 0]
    section_count = coef_all.shape[0]
    for level in range(section_count):
        partner_image = from_partner(level_image, "sub", level % bit_count)
        level_image = merge_level(
            level_image, partner_image, coef_all[level], start_all[level], width_all[level]
        )
    return level_image[:, :, None, :]


def solution(mesh):
    return jax.shard_map(
        on_device,
        mesh=mesh,
        in_specs=(
            P(None, "sub", "section", "rng"),
            P(),
            P(None, "sub", None, None),
            P("sub", None),
            P(None, "sub", None, None, None, None),
            P(None, "sub", None, None),
            P(None, "sub", None, None),
        ),
        out_specs=P(None, "sub", "rng", "section"),
        check_vma=False,
    )
```

profile of v0, /device:TPU:1, one launch (start us, length us, event | category | flops | bytes accessed | tf_op | source)
XLA Modules:
  0.0 180.4 jit_solution(6251457165325808575)
XLA Ops:
  0.0 1.5 slice.437
  1.5 8.8 %collective-permute-start = (bf16[2,6,2048]{2,0,1:T(2,128)(2,1)}, bf16[2,6,2048]{2,0,1:T(2,128)(2,1)}, u32[]{:S(2)}, u32[]{:S(2)}) collective-permute-start(bf16[2,6,2048]{2,0,1:T(2,128)(2,1)} %slice.437), channel_id=1, source_target_pairs={{1,0},{2,1},{3,2},{5,4},{6,5},{7,6},{9,8},{10,9},{11,10},{13,12},{... | collective-permute-start | bytes 147464 | tf_op jit(solution)/shard_map/ppermute | solution.py:12
  11.1 1.3 copy.173
  12.4 0.9 slice.438
  13.3 2.1 %reshape.582 = bf16[622336]{0:T(1024)(128)(2,1)S(1)} reshape(bf16[2,311168]{1,0:T(2,128)(2,1)S(1)} %slice.438) | data formatting | bytes 2489344
  15.5 2.2 %reshape.578 = bf16[2,128,2431]{2,1,0:T(8,128)(2,1)S(1)} reshape(bf16[622336]{0:T(1024)(128)(2,1)S(1)} %reshape.582) | data formatting | bytes 2489344 | tf_op jit(solution)/shard_map/reshape | solution.py:62
  17.7 1.1 slice.439
  18.7 1.7 copy.133
  20.6 0.9 fusion.186
  25.3 0.7 fusion.208
  33.1 0.7 fusion.204
  34.5 0.8 iota_subtract_fusion.6
  35.3 1.4 maximum_maximum_fusion
  36.7 1.1 maximum_bitcast_fusion
  37.9 4.0 %while.14 = (s32[]{:T(128)}, f32[6,32,256]{2,1,0:T(8,128)S(1)}, bf16[6,48,256]{2,1,0:T(8,128)(2,1)S(1)}, bf16[17,256,256]{2,1,0:T(8,128)(2,1)S(1)}, s32[]{:T(128)}, /*index=5*/s32[]{:T(128)}) while((s32[]{:T(128)}, f32[6,32,256]{2,1,0:T(8,128)S(1)}, bf16[6,48,256]{2,1,0:T(8,128)(2,1)S(1)}, bf16[17,256,256]{2,1,0:T(8,128)(2,1)S(1)}, ...), condition=%wide.region_1.2_spmd.clone, body=%wide.region_0.1_spmd.clone.sunk | while | flops 25264132 | bytes 623695 | solution.py:93
  41.9 1.4 copy.140
  43.3 4.2 %reshape.584 = bf16[4,2,6144]{2,1,0:T(2,128)(2,1)} reshape(bf16[4096,2,6]{2,1,0:T(2,128)(2,1)S(1)} %bitcast.228) | data formatting | bytes 196608
  47.5 3.5 %all-to-all-start = ((bf16[4,2,6144]{2,1,0:T(2,128)(2,1)}), bf16[4,2,6144]{2,1,0:T(2,128)(2,1)S(1)}, u32[]{:S(2)}, u32[]{:S(2)}) async-start(bf16[4,2,6144]{2,1,0:T(2,128)(2,1)} %reshape.584), calls=%async_computation | async-start | bytes 196608 | tf_op jit(solution)/shard_map/all_to_all | solution.py:106
  51.0 4.9 %all-to-all-done = bf16[4,2,6144]{2,1,0:T(2,128)(2,1)S(1)} async-done(((bf16[4,2,6144]{2,1,0:T(2,128)(2,1)}), bf16[4,2,6144]{2,1,0:T(2,128)(2,1)S(1)}, u32[]{:S(2)}, u32[]{:S(2)}) %all-to-all-start) | async-done | bytes 98336 | tf_op jit(solution)/shard_map/all_to_all | solution.py:106
  55.9 4.8 %reshape.585 = bf16[4096,2,6]{2,1,0:T(2,128)(2,1)S(1)} reshape(bf16[4,2,6144]{2,1,0:T(2,128)(2,1)S(1)} %all-to-all-done) | data formatting | bytes 196608
  60.7 1.5 copy.141
  62.8 1.9 %collective-permute-start.1 = (bf16[2,128,1024]{2,1,0:T(8,128)(2,1)S(1)}, bf16[2,128,1024]{2,1,0:T(8,128)(2,1)S(1)}, u32[]{:S(2)}, u32[]{:S(2)}) collective-permute-start(bf16[2,128,1024]{2,1,0:T(8,128)(2,1)S(1)} %bitcast.233), channel_id=1, source_target_pairs={{0,4},{4,0},{8,12},{12,8},{16,20},{20,16},{24,28},{28,24},{32,36},... | collective-permute-start | bytes 1572872 | tf_op jit(solution)/shard_map/ppermute | solution.py:22
  65.6 12.2 %collective-permute-done.1 = bf16[2,128,1024]{2,1,0:T(8,128)(2,1)S(1)} collective-permute-done((bf16[2,128,1024]{2,1,0:T(8,128)(2,1)S(1)}, bf16[2,128,1024]{2,1,0:T(8,128)(2,1)S(1)}, u32[]{:S(2)}, u32[]{:S(2)}) %collective-permute-start.1) | collective-permute-done | bytes 524320 | tf_op jit(solution)/shard_map/ppermute | solution.py:22
  78.4 2.1 %collective-permute-start.2 = (bf16[2,128,1024]{2,1,0:T(8,128)(2,1)S(1)}, bf16[2,128,1024]{2,1,0:T(8,128)(2,1)S(1)}, u32[]{:S(2)}, u32[]{:S(2)}) collective-permute-start(bf16[2,128,1024]{2,1,0:T(8,128)(2,1)S(1)} %bitcast.247), channel_id=1, source_target_pairs={{0,8},{8,0},{4,12},{12,4},{16,24},{24,16},{20,28},{28,20},{32,40},... | collective-permute-start | bytes 1572872 | tf_op jit(solution)/shard_map/ppermute | solution.py:22
  81.2 25.1 %collective-permute-done.2 = bf16[2,128,1024]{2,1,0:T(8,128)(2,1)S(1)} collective-permute-done((bf16[2,128,1024]{2,1,0:T(8,128)(2,1)S(1)}, bf16[2,128,1024]{2,1,0:T(8,128)(2,1)S(1)}, u32[]{:S(2)}, u32[]{:S(2)}) %collective-permute-start.2) | collective-permute-done | bytes 524320 | tf_op jit(solution)/shard_map/ppermute | solution.py:22
  107.0 3.0 %collective-permute-start.3 = (bf16[2,128,1024]{2,1,0:T(8,128)(2,1)S(1)}, bf16[2,128,1024]{2,1,0:T(8,128)(2,1)S(1)}, u32[]{:S(2)}, u32[]{:S(2)}) collective-permute-start(bf16[2,128,1024]{2,1,0:T(8,128)(2,1)S(1)} %bitcast.248), channel_id=1, source_target_pairs={{0,16},{16,0},{4,20},{20,4},{8,24},{24,8},{12,28},{28,12},{32,48},... | collective-permute-start | bytes 1572872 | tf_op jit(solution)/shard_map/ppermute | solution.py:22
  110.8 24.9 %collective-permute-done.3 = bf16[2,128,1024]{2,1,0:T(8,128)(2,1)S(1)} collective-permute-done((bf16[2,128,1024]{2,1,0:T(8,128)(2,1)S(1)}, bf16[2,128,1024]{2,1,0:T(8,128)(2,1)S(1)}, u32[]{:S(2)}, u32[]{:S(2)}) %collective-permute-start.3) | collective-permute-done | bytes 524320 | tf_op jit(solution)/shard_map/ppermute | solution.py:22
  136.2 1.9 %collective-permute-start.4 = (bf16[2,128,1024]{2,1,0:T(8,128)(2,1)S(1)}, bf16[2,128,1024]{2,1,0:T(8,128)(2,1)S(1)}, u32[]{:S(2)}, u32[]{:S(2)}) collective-permute-start(bf16[2,128,1024]{2,1,0:T(8,128)(2,1)S(1)} %bitcast.249), channel_id=1, source_target_pairs={{0,32},{32,0},{4,36},{36,4},{8,40},{40,8},{12,44},{44,12},{16,48},... | collective-permute-start | bytes 1572872 | tf_op jit(solution)/shard_map/ppermute | solution.py:22
  138.9 11.9 %collective-permute-done.4 = bf16[2,128,1024]{2,1,0:T(8,128)(2,1)S(1)} collective-permute-done((bf16[2,128,1024]{2,1,0:T(8,128)(2,1)S(1)}, bf16[2,128,1024]{2,1,0:T(8,128)(2,1)S(1)}, u32[]{:S(2)}, u32[]{:S(2)}) %collective-permute-start.4) | collective-permute-done | bytes 524320 | tf_op jit(solution)/shard_map/ppermute | solution.py:22
  151.4 3.2 %collective-permute-start.5 = (bf16[2,128,1024]{2,1,0:T(8,128)(2,1)S(1)}, bf16[2,128,1024]{2,1,0:T(8,128)(2,1)S(1)}, u32[]{:S(2)}, u32[]{:S(2)}) collective-permute-start(bf16[2,128,1024]{2,1,0:T(8,128)(2,1)S(1)} %bitcast.250), channel_id=1, source_target_pairs={{0,64},{64,0},{4,68},{68,4},{8,72},{72,8},{12,76},{76,12},{16,80},... | collective-permute-start | bytes 1572872 | tf_op jit(solution)/shard_map/ppermute | solution.py:22
  154.8 24.4 %collective-permute-done.5 = bf16[2,128,1024]{2,1,0:T(8,128)(2,1)S(1)} collective-permute-done((bf16[2,128,1024]{2,1,0:T(8,128)(2,1)S(1)}, bf16[2,128,1024]{2,1,0:T(8,128)(2,1)S(1)}, u32[]{:S(2)}, u32[]{:S(2)}) %collective-permute-start.5) | collective-permute-done | bytes 524320 | tf_op jit(solution)/shard_map/ppermute | solution.py:22
  179.2 1.2 convolution_convert_fusion
  (176 shorter events, 21.8 us)
Async XLA Ops:
  0.0 26.7 %copy-start = (bf16[2,1,128,24]{2,3,1,0:T(8,128)(2,1)S(1)}, bf16[2,1,128,24]{2,3,1,0:T(8,128)(2,1)}, u32[]{:S(2)}) copy-start(bf16[2,1,128,24]{2,3,1,0:T(8,128)(2,1)} %param.11) | copy-start | bytes 36868
  1.5 35.3 %collective-permute-start = (bf16[2,6,2048]{2,0,1:T(2,128)(2,1)}, bf16[2,6,2048]{2,0,1:T(2,128)(2,1)}, u32[]{:S(2)}, u32[]{:S(2)}) collective-permute-start(bf16[2,6,2048]{2,0,1:T(2,128)(2,1)} %slice.437), channel_id=1, source_target_pairs={{1,0},{2,1},{3,2},{5,4},{6,5},{7,6},{9,8},{10,9},{11,10},{13,12},{... | collective-permute-start | bytes 147464 | tf_op jit(solution)/shard_map/ppermute | solution.py:12
  21.5 5.2 %copy-start.34 = (s32[1,24]{1,0:T(1,128)S(1)}, s32[1,24]{1,0:T(1,128)}, u32[]{:S(2)}) copy-start(s32[1,24]{1,0:T(1,128)} %param.12) | copy-start | bytes 292
  26.9 4.2 %copy-start.23 = (bf16[2,128,24]{1,2,0:T(8,128)(2,1)}, bf16[2,128,24]{1,2,0:T(8,128)(2,1)S(1)}, u32[]{:S(2)}) copy-start(bf16[2,128,24]{1,2,0:T(8,128)(2,1)S(1)} %fusion.14) | copy-start | bytes 36868
  41.9 9.0 %copy-start.24 = (bf16[2,128,24]{1,2,0:T(8,128)(2,1)S(1)}, bf16[2,128,24]{1,2,0:T(8,128)(2,1)}, u32[]{:S(2)}) copy-start(bf16[2,128,24]{1,2,0:T(8,128)(2,1)} %copy-done.23) | copy-start | bytes 36868
  47.5 8.4 %all-to-all-start = ((bf16[4,2,6144]{2,1,0:T(2,128)(2,1)}), bf16[4,2,6144]{2,1,0:T(2,128)(2,1)S(1)}, u32[]{:S(2)}, u32[]{:S(2)}) async-start(bf16[4,2,6144]{2,1,0:T(2,128)(2,1)} %reshape.584), calls=%async_computation | async-start | bytes 196608 | tf_op jit(solution)/shard_map/all_to_all | solution.py:106
  51.0 11.4 %copy-start.25 = (bf16[128,24]{0,1:T(8,128)(2,1)S(1)}, bf16[128,24]{0,1:T(8,128)(2,1)}, u32[]{:S(2)}) copy-start(bf16[128,24]{0,1:T(8,128)(2,1)} %get-tuple-element.172) | copy-start | bytes 18436
  51.0 11.4 %copy-start.26 = (bf16[128,24]{0,1:T(8,128)(2,1)S(1)}, bf16[128,24]{0,1:T(8,128)(2,1)}, u32[]{:S(2)}) copy-start(bf16[128,24]{0,1:T(8,128)(2,1)} %get-tuple-element.173) | copy-start | bytes 18436
  60.6 4.0 %copy-start.32 = (s32[128]{0:T(128)S(1)}, s32[128]{0:T(128)}, u32[]{:S(2)}) copy-start(s32[128]{0:T(128)} %get-tuple-element.179) | copy-start | bytes 1540
  60.7 4.0 %copy-start.33 = (s32[128]{0:T(128)S(1)}, s32[128]{0:T(128)}, u32[]{:S(2)}) copy-start(s32[128]{0:T(128)} %get-tuple-element.180) | copy-start | bytes 1540
  60.7 4.2 %copy-start.2 = (bf16[1,128,128]{2,0,1:T(2,128)(2,1)S(1)}, bf16[1,128,128]{2,0,1:T(2,128)(2,1)}, u32[]{:S(2)}) copy-start(bf16[1,128,128]{2,0,1:T(2,128)(2,1)} %get-tuple-element.171) | copy-start | bytes 98308
  60.7 4.2 %copy-start.10 = (bf16[1,1,1,2,128,16]{4,5,3,2,1,0:T(8,128)(2,1)S(1)}, bf16[1,1,1,2,128,16]{4,5,3,2,1,0:T(8,128)(2,1)}, u32[]{:S(2)}) copy-start(bf16[1,1,1,2,128,16]{4,5,3,2,1,0:T(8,128)(2,1)} %get-tuple-element.149) | copy-start | bytes 24580
  60.7 4.3 %copy-start.6 = (s32[128,128]{1,0:T(8,128)S(1)}, s32[128,128]{1,0:T(8,128)}, u32[]{:S(2)}) copy-start(s32[128,128]{1,0:T(8,128)} %get-tuple-element.201) | copy-start | bytes 196612
  62.2 15.6 %copy-start.15 = (bf16[128,128]{1,0:T(8,128)(2,1)S(1)}, bf16[128,128]{1,0:T(8,128)(2,1)}, u32[]{:S(2)}) copy-start(bf16[128,128]{1,0:T(8,128)(2,1)} %get-tuple-element.124) | copy-start | bytes 98308
  62.2 15.6 %copy-start.16 = (bf16[128,128]{1,0:T(8,128)(2,1)S(1)}, bf16[128,128]{1,0:T(8,128)(2,1)}, u32[]{:S(2)}) copy-start(bf16[128,128]{1,0:T(8,128)(2,1)} %get-tuple-element.125) | copy-start | bytes 98308
  62.2 15.6 %copy-start.21 = (bf16[128,128]{1,0:T(8,128)(2,1)S(1)}, bf16[128,128]{1,0:T(8,128)(2,1)}, u32[]{:S(2)}) copy-start(bf16[128,128]{1,0:T(8,128)(2,1)} %get-tuple-element.126) | copy-start | bytes 98308
  62.3 15.6 %copy-start.22 = (bf16[128,128]{1,0:T(8,128)(2,1)S(1)}, bf16[128,128]{1,0:T(8,128)(2,1)}, u32[]{:S(2)}) copy-start(bf16[128,128]{1,0:T(8,128)(2,1)} %get-tuple-element.127) | copy-start | bytes 98308
  62.8 15.0 %collective-permute-start.1 = (bf16[2,128,1024]{2,1,0:T(8,128)(2,1)S(1)}, bf16[2,128,1024]{2,1,0:T(8,128)(2,1)S(1)}, u32[]{:S(2)}, u32[]{:S(2)}) collective-permute-start(bf16[2,128,1024]{2,1,0:T(8,128)(2,1)S(1)} %bitcast.233), channel_id=1, source_target_pairs={{0,4},{4,0},{8,12},{12,8},{16,20},{20,16},{24,28},{28,24},{32,36},... | collective-permute-start | bytes 1572872 | tf_op jit(solution)/shard_map/ppermute | solution.py:22
  78.3 28.0 %copy-start.13 = (bf16[128,128]{1,0:T(8,128)(2,1)S(1)}, bf16[128,128]{1,0:T(8,128)(2,1)}, u32[]{:S(2)}) copy-start(bf16[128,128]{1,0:T(8,128)(2,1)} %get-tuple-element.120) | copy-start | bytes 98308
  78.4 28.0 %copy-start.14 = (bf16[128,128]{1,0:T(8,128)(2,1)S(1)}, bf16[128,128]{1,0:T(8,128)(2,1)}, u32[]{:S(2)}) copy-start(bf16[128,128]{1,0:T(8,128)(2,1)} %get-tuple-element.121) | copy-start | bytes 98308
  78.4 28.0 %copy-start.19 = (bf16[128,128]{1,0:T(8,128)(2,1)S(1)}, bf16[128,128]{1,0:T(8,128)(2,1)}, u32[]{:S(2)}) copy-start(bf16[128,128]{1,0:T(8,128)(2,1)} %get-tuple-element.122) | copy-start | bytes 98308
  78.4 28.0 %copy-start.20 = (bf16[128,128]{1,0:T(8,128)(2,1)S(1)}, bf16[128,128]{1,0:T(8,128)(2,1)}, u32[]{:S(2)}) copy-start(bf16[128,128]{1,0:T(8,128)(2,1)} %get-tuple-element.123) | copy-start | bytes 98308
  78.4 28.0 %collective-permute-start.2 = (bf16[2,128,1024]{2,1,0:T(8,128)(2,1)S(1)}, bf16[2,128,1024]{2,1,0:T(8,128)(2,1)S(1)}, u32[]{:S(2)}, u32[]{:S(2)}) collective-permute-start(bf16[2,128,1024]{2,1,0:T(8,128)(2,1)S(1)} %bitcast.247), channel_id=1, source_target_pairs={{0,8},{8,0},{4,12},{12,4},{16,24},{24,16},{20,28},{28,20},{32,40},... | collective-permute-start | bytes 1572872 | tf_op jit(solution)/shard_map/ppermute | solution.py:22
  106.4 3.6 %copy-start.1 = (bf16[1,128,128]{2,0,1:T(2,128)(2,1)S(1)}, bf16[1,128,128]{2,0,1:T(2,128)(2,1)}, u32[]{:S(2)}) copy-start(bf16[1,128,128]{2,0,1:T(2,128)(2,1)} %get-tuple-element.163) | copy-start | bytes 98308
  106.4 3.6 %copy-start.8 = (bf16[1,1,1,2,128,16]{4,5,3,2,1,0:T(8,128)(2,1)S(1)}, bf16[1,1,1,2,128,16]{4,5,3,2,1,0:T(8,128)(2,1)}, u32[]{:S(2)}) copy-start(bf16[1,1,1,2,128,16]{4,5,3,2,1,0:T(8,128)(2,1)} %get-tuple-element.142) | copy-start | bytes 24580
  106.9 28.8 %copy-start.11 = (bf16[128,128]{1,0:T(8,128)(2,1)S(1)}, bf16[128,128]{1,0:T(8,128)(2,1)}, u32[]{:S(2)}) copy-start(bf16[128,128]{1,0:T(8,128)(2,1)} %get-tuple-element.116) | copy-start | bytes 98308
  106.9 28.8 %copy-start.12 = (bf16[128,128]{1,0:T(8,128)(2,1)S(1)}, bf16[128,128]{1,0:T(8,128)(2,1)}, u32[]{:S(2)}) copy-start(bf16[128,128]{1,0:T(8,128)(2,1)} %get-tuple-element.117) | copy-start | bytes 98308
  106.9 28.8 %copy-start.17 = (bf16[128,128]{1,0:T(8,128)(2,1)S(1)}, bf16[128,128]{1,0:T(8,128)(2,1)}, u32[]{:S(2)}) copy-start(bf16[128,128]{1,0:T(8,128)(2,1)} %get-tuple-element.118) | copy-start | bytes 98308
  106.9 28.8 %copy-start.18 = (bf16[128,128]{1,0:T(8,128)(2,1)S(1)}, bf16[128,128]{1,0:T(8,128)(2,1)}, u32[]{:S(2)}) copy-start(bf16[128,128]{1,0:T(8,128)(2,1)} %get-tuple-element.119) | copy-start | bytes 98308
  107.0 28.7 %collective-permute-start.3 = (bf16[2,128,1024]{2,1,0:T(8,128)(2,1)S(1)}, bf16[2,128,1024]{2,1,0:T(8,128)(2,1)S(1)}, u32[]{:S(2)}, u32[]{:S(2)}) collective-permute-start(bf16[2,128,1024]{2,1,0:T(8,128)(2,1)S(1)} %bitcast.248), channel_id=1, source_target_pairs={{0,16},{16,0},{4,20},{20,4},{8,24},{24,8},{12,28},{28,12},{32,48},... | collective-permute-start | bytes 1572872 | tf_op jit(solution)/shard_map/ppermute | solution.py:22
  136.2 14.6 %collective-permute-start.4 = (bf16[2,128,1024]{2,1,0:T(8,128)(2,1)S(1)}, bf16[2,128,1024]{2,1,0:T(8,128)(2,1)S(1)}, u32[]{:S(2)}, u32[]{:S(2)}) collective-permute-start(bf16[2,128,1024]{2,1,0:T(8,128)(2,1)S(1)} %bitcast.249), channel_id=1, source_target_pairs={{0,32},{32,0},{4,36},{36,4},{8,40},{40,8},{12,44},{44,12},{16,48},... | collective-permute-start | bytes 1572872 | tf_op jit(solution)/shard_map/ppermute | solution.py:22
  151.4 27.8 %collective-permute-start.5 = (bf16[2,128,1024]{2,1,0:T(8,128)(2,1)S(1)}, bf16[2,128,1024]{2,1,0:T(8,128)(2,1)S(1)}, u32[]{:S(2)}, u32[]{:S(2)}) collective-permute-start(bf16[2,128,1024]{2,1,0:T(8,128)(2,1)S(1)} %bitcast.250), channel_id=1, source_target_pairs={{0,64},{64,0},{4,68},{68,4},{8,72},{72,8},{12,76},{76,12},{16,80},... | collective-permute-start | bytes 1572872 | tf_op jit(solution)/shard_map/ppermute | solution.py:22
  (10 other events, 24.4 us)
where the time goes:
time: 181 us; the launch traced here: 180 us
  waiting for transfers between devices  103 us (57%)
  local copies, waits for them, and re-layouts  29.8 us (16%)
  starting transfers between devices  24.3 us (13%)
  matrix products  11.7 us (6%)
  other arithmetic  9.67 us (5%)
    ppermute x5, waiting for transfers between devices, from_partner(): return lax.ppermute(block, axis, route)  98.5 us
    unnamed x95, local copies, waits for them, and re-layouts  13.9 us
    ppermute x5, starting transfers between devices, from_partner(): return lax.ppermute(block, axis, route)  12.1 us
    ppermute x1, starting transfers between devices, from_behind(): return lax.ppermute(value, axis, pairs)  8.78 us
    all_to_all x1, waiting for transfers between devices, on_device(): lax.all_to_all(compressed, 'section', split_axis=2, concat_axis=1, tiled=...  4.89 us
    dot_general x10, matrix products, band_matrix(): jnp.einsum('sqt,tqc->sqc', coef_side, selector, preferred_element_type=jn...  4.58 us
  transfers between devices with their start and end apart: 7, of which 6 were waited for; matrix products, arithmetic and copies ran while one was open for 16% of the time, Pallas kernels for 0%

commit v1 on v0

--- a/solution.py
+++ b/solution.py
@@ -103,7 +103,9 @@
 
 def on_device(echoes, chirp, steer, pulse_order, band_coef, band_start, band_width):
     compressed = compress(echoes[:, 0], chirp)
-    pulse_rows = lax.all_to_all(compressed, "section", split_axis=2, concat_axis=1, tiled=True)
+    cells = jnp.split(compressed, lax.axis_size("section"), axis=2)
+    received = lax.all_to_all(jnp.stack(cells), "section", 0, 0)
+    pulse_rows = jnp.concatenate(received, axis=1)
     position_count = pulse_order.shape[1]
     positions = jnp.arange(position_count, dtype=jnp.int32)
     selector = (positions[:, None] == pulse_order[0][None, :]).astype(jnp.bfloat16)

time: 181 us -> 171 us (0.945)
  local copies, waits for them, and re-layouts: 29.8 us -> 18.5 us
    unnamed x95 -> x93, local copies, waits for them, and re-layouts: 13.9 us -> 4.97 us
  transfers between devices with their start and end apart: 7 -> 7, of which waited for: 6 -> 6; matrix products, arithmetic and copies ran while one was open for 16% -> 17% of each run, Pallas kernels for 0% -> 0%
where the time goes in v1:
time: 171 us; the launch traced here: 170 us
  waiting for transfers between devices  103 us (60%)
  starting transfers between devices  24.5 us (14%)
  local copies, waits for them, and re-layouts  18.5 us (11%)
  matrix products  11.7 us (7%)
  other arithmetic  10.5 us (6%)
    ppermute x5, waiting for transfers between devices, from_partner(): return lax.ppermute(block, axis, route)  98.4 us
    ppermute x5, starting transfers between devices, from_partner(): return lax.ppermute(block, axis, route)  12.1 us
    ppermute x1, starting transfers between devices, from_behind(): return lax.ppermute(value, axis, pairs)  8.78 us
    unnamed x93, local copies, waits for them, and re-layouts  4.97 us
    all_to_all x1, waiting for transfers between devices, on_device(): received = lax.all_to_all(jnp.stack(cells), 'section', 0, 0)  4.92 us
    dot_general x10, matrix products, band_matrix(): jnp.einsum('sqt,tqc->sqc', coef_side, selector, preferred_element_type=jn...  4.58 us
    all_to_all x1, starting transfers between devices, on_device(): received = lax.all_to_all(jnp.stack(cells), 'section', 0, 0)  3.63 us
    dot_general x17, matrix products, add_piece(): jnp.einsum('pbi,io->pbo', window, table, preferred_element_type=jnp.float32)  3.56 us
  transfers between devices with their start and end apart: 7, of which 6 were waited for; matrix products, arithmetic and copies ran while one was open for 17% of the time, Pallas kernels for 0%

profile of v1, /device:TPU:1, one launch (start us, length us, event | category | flops | bytes accessed | tf_op | source)
XLA Modules:
  0.0 169.9 jit_solution(12096952095010586408)
XLA Ops:
  0.0 1.5 slice.437
  1.5 8.8 %collective-permute-start = (bf16[2,6,2048]{2,0,1:T(2,128)(2,1)}, bf16[2,6,2048]{2,0,1:T(2,128)(2,1)}, u32[]{:S(2)}, u32[]{:S(2)}) collective-permute-start(bf16[2,6,2048]{2,0,1:T(2,128)(2,1)} %slice.437), channel_id=1, source_target_pairs={{1,0},{2,1},{3,2},{5,4},{6,5},{7,6},{9,8},{10,9},{11,10},{13,12},{... | collective-permute-start | bytes 147464 | tf_op jit(solution)/shard_map/ppermute | solution.py:12
  10.3 0.7 maximum_maximum_fusion.1
  11.1 1.3 copy.129
  12.4 0.9 slice.438
  13.3 2.1 %reshape.589 = bf16[622336]{0:T(1024)(128)(2,1)S(1)} reshape(bf16[2,311168]{1,0:T(2,128)(2,1)S(1)} %slice.438) | data formatting | bytes 2489344
  15.5 2.2 %reshape.582 = bf16[2,128,2431]{2,1,0:T(8,128)(2,1)S(1)} reshape(bf16[622336]{0:T(1024)(128)(2,1)S(1)} %reshape.589) | data formatting | bytes 2489344 | tf_op jit(solution)/shard_map/reshape | solution.py:62
  17.7 1.1 slice.439
  18.7 1.7 copy.93
  20.6 0.9 fusion.186
  26.2 0.7 fusion.207
  29.7 0.7 fusion.205
  33.2 0.7 fusion.203
  33.9 0.7 fusion.192
  34.6 0.8 iota_subtract_fusion.6
  35.3 1.4 maximum_maximum_fusion
  36.8 1.1 maximum_bitcast_fusion
  38.0 4.0 %while.14 = (s32[]{:T(128)}, f32[6,32,256]{2,1,0:T(8,128)S(1)}, bf16[6,48,256]{2,1,0:T(8,128)(2,1)S(1)}, bf16[17,256,256]{2,1,0:T(8,128)(2,1)S(1)}, s32[]{:T(128)}, /*index=5*/s32[]{:T(128)}) while((s32[]{:T(128)}, f32[6,32,256]{2,1,0:T(8,128)S(1)}, bf16[6,48,256]{2,1,0:T(8,128)(2,1)S(1)}, bf16[17,256,256]{2,1,0:T(8,128)(2,1)S(1)}, ...), condition=%wide.region_1.2_spmd.clone, body=%wide.region_0.1_spmd.clone.sunk | while | flops 25264132 | bytes 623695 | solution.py:93
  42.2 0.8 pad_maximum_fusion
  43.0 3.6 %all-to-all-start = ((bf16[4,2,6,1024]{3,1,2,0:T(2,128)(2,1)}), bf16[4,2,6,1024]{3,1,2,0:T(2,128)(2,1)S(1)}, u32[]{:S(2)}, u32[]{:S(2)}) async-start(bf16[4,2,6,1024]{3,1,2,0:T(2,128)(2,1)} %pad_maximum_fusion), calls=%async_computation | async-start | bytes 196608 | tf_op jit(solution)/shard_map/all_to_all | solution.py:107
  46.6 4.9 %all-to-all-done = bf16[4,2,6,1024]{3,1,2,0:T(2,128)(2,1)S(1)} async-done(((bf16[4,2,6,1024]{3,1,2,0:T(2,128)(2,1)}), bf16[4,2,6,1024]{3,1,2,0:T(2,128)(2,1)S(1)}, u32[]{:S(2)}, u32[]{:S(2)}) %all-to-all-start) | async-done | bytes 98336 | tf_op jit(solution)/shard_map/all_to_all | solution.py:107
  52.4 1.9 %collective-permute-start.1 = (bf16[2,128,1024]{2,1,0:T(8,128)(2,1)S(1)}, bf16[2,128,1024]{2,1,0:T(8,128)(2,1)S(1)}, u32[]{:S(2)}, u32[]{:S(2)}) collective-permute-start(bf16[2,128,1024]{2,1,0:T(8,128)(2,1)S(1)} %bitcast.240), channel_id=1, source_target_pairs={{0,4},{4,0},{8,12},{12,8},{16,20},{20,16},{24,28},{28,24},{32,36},... | collective-permute-start | bytes 1572872 | tf_op jit(solution)/shard_map/ppermute | solution.py:22
  55.2 12.2 %collective-permute-done.1 = bf16[2,128,1024]{2,1,0:T(8,128)(2,1)S(1)} collective-permute-done((bf16[2,128,1024]{2,1,0:T(8,128)(2,1)S(1)}, bf16[2,128,1024]{2,1,0:T(8,128)(2,1)S(1)}, u32[]{:S(2)}, u32[]{:S(2)}) %collective-permute-start.1) | collective-permute-done | bytes 524320 | tf_op jit(solution)/shard_map/ppermute | solution.py:22
  68.0 2.1 %collective-permute-start.2 = (bf16[2,128,1024]{2,1,0:T(8,128)(2,1)S(1)}, bf16[2,128,1024]{2,1,0:T(8,128)(2,1)S(1)}, u32[]{:S(2)}, u32[]{:S(2)}) collective-permute-start(bf16[2,128,1024]{2,1,0:T(8,128)(2,1)S(1)} %bitcast.253), channel_id=1, source_target_pairs={{0,8},{8,0},{4,12},{12,4},{16,24},{24,16},{20,28},{28,20},{32,40},... | collective-permute-start | bytes 1572872 | tf_op jit(solution)/shard_map/ppermute | solution.py:22
  70.9 25.1 %collective-permute-done.2 = bf16[2,128,1024]{2,1,0:T(8,128)(2,1)S(1)} collective-permute-done((bf16[2,128,1024]{2,1,0:T(8,128)(2,1)S(1)}, bf16[2,128,1024]{2,1,0:T(8,128)(2,1)S(1)}, u32[]{:S(2)}, u32[]{:S(2)}) %collective-permute-start.2) | collective-permute-done | bytes 524320 | tf_op jit(solution)/shard_map/ppermute | solution.py:22
  96.6 2.9 %collective-permute-start.3 = (bf16[2,128,1024]{2,1,0:T(8,128)(2,1)S(1)}, bf16[2,128,1024]{2,1,0:T(8,128)(2,1)S(1)}, u32[]{:S(2)}, u32[]{:S(2)}) collective-permute-start(bf16[2,128,1024]{2,1,0:T(8,128)(2,1)S(1)} %bitcast.254), channel_id=1, source_target_pairs={{0,16},{16,0},{4,20},{20,4},{8,24},{24,8},{12,28},{28,12},{32,48},... | collective-permute-start | bytes 1572872 | tf_op jit(solution)/shard_map/ppermute | solution.py:22
  100.4 24.9 %collective-permute-done.3 = bf16[2,128,1024]{2,1,0:T(8,128)(2,1)S(1)} collective-permute-done((bf16[2,128,1024]{2,1,0:T(8,128)(2,1)S(1)}, bf16[2,128,1024]{2,1,0:T(8,128)(2,1)S(1)}, u32[]{:S(2)}, u32[]{:S(2)}) %collective-permute-start.3) | collective-permute-done | bytes 524320 | tf_op jit(solution)/shard_map/ppermute | solution.py:22
  125.8 1.9 %collective-permute-start.4 = (bf16[2,128,1024]{2,1,0:T(8,128)(2,1)S(1)}, bf16[2,128,1024]{2,1,0:T(8,128)(2,1)S(1)}, u32[]{:S(2)}, u32[]{:S(2)}) collective-permute-start(bf16[2,128,1024]{2,1,0:T(8,128)(2,1)S(1)} %bitcast.255), channel_id=1, source_target_pairs={{0,32},{32,0},{4,36},{36,4},{8,40},{40,8},{12,44},{44,12},{16,48},... | collective-permute-start | bytes 1572872 | tf_op jit(solution)/shard_map/ppermute | solution.py:22
  128.4 11.9 %collective-permute-done.4 = bf16[2,128,1024]{2,1,0:T(8,128)(2,1)S(1)} collective-permute-done((bf16[2,128,1024]{2,1,0:T(8,128)(2,1)S(1)}, bf16[2,128,1024]{2,1,0:T(8,128)(2,1)S(1)}, u32[]{:S(2)}, u32[]{:S(2)}) %collective-permute-start.4) | collective-permute-done | bytes 524320 | tf_op jit(solution)/shard_map/ppermute | solution.py:22
  140.8 3.3 %collective-permute-start.5 = (bf16[2,128,1024]{2,1,0:T(8,128)(2,1)S(1)}, bf16[2,128,1024]{2,1,0:T(8,128)(2,1)S(1)}, u32[]{:S(2)}, u32[]{:S(2)}) collective-permute-start(bf16[2,128,1024]{2,1,0:T(8,128)(2,1)S(1)} %bitcast.256), channel_id=1, source_target_pairs={{0,64},{64,0},{4,68},{68,4},{8,72},{72,8},{12,76},{76,12},{16,80},... | collective-permute-start | bytes 1572872 | tf_op jit(solution)/shard_map/ppermute | solution.py:22
  144.3 24.3 %collective-permute-done.5 = bf16[2,128,1024]{2,1,0:T(8,128)(2,1)S(1)} collective-permute-done((bf16[2,128,1024]{2,1,0:T(8,128)(2,1)S(1)}, bf16[2,128,1024]{2,1,0:T(8,128)(2,1)S(1)}, u32[]{:S(2)}, u32[]{:S(2)}) %collective-permute-start.5) | collective-permute-done | bytes 524320 | tf_op jit(solution)/shard_map/ppermute | solution.py:22
  168.7 1.2 convolution_convert_fusion
  (173 shorter events, 20.2 us)
Async XLA Ops:
  0.0 21.5 %copy-start = (bf16[2,1,128,24]{2,3,1,0:T(8,128)(2,1)S(1)}, bf16[2,1,128,24]{2,3,1,0:T(8,128)(2,1)}, u32[]{:S(2)}) copy-start(bf16[2,1,128,24]{2,3,1,0:T(8,128)(2,1)} %param.11) | copy-start | bytes 36868
  1.5 35.3 %collective-permute-start = (bf16[2,6,2048]{2,0,1:T(2,128)(2,1)}, bf16[2,6,2048]{2,0,1:T(2,128)(2,1)}, u32[]{:S(2)}, u32[]{:S(2)}) collective-permute-start(bf16[2,6,2048]{2,0,1:T(2,128)(2,1)} %slice.437), channel_id=1, source_target_pairs={{1,0},{2,1},{3,2},{5,4},{6,5},{7,6},{9,8},{10,9},{11,10},{13,12},{... | collective-permute-start | bytes 147464 | tf_op jit(solution)/shard_map/ppermute | solution.py:12
  20.5 3.0 %copy-start.4 = (bf16[5,1,2,2,128,16]{4,5,3,2,1,0:T(8,128)(2,1)S(1)}, bf16[5,1,2,2,128,16]{4,5,3,2,1,0:T(8,128)(2,1)}, u32[]{:S(2)}) copy-start(bf16[5,1,2,2,128,16]{4,5,3,2,1,0:T(8,128)(2,1)} %param.13) | copy-start | bytes 245764
  38.0 8.7 %copy-start.24 = (bf16[2,128,24]{1,2,0:T(8,128)(2,1)S(1)}, bf16[2,128,24]{1,2,0:T(8,128)(2,1)}, u32[]{:S(2)}) copy-start(bf16[2,128,24]{1,2,0:T(8,128)(2,1)} %copy-done.23) | copy-start | bytes 36868
  38.0 14.1 %copy-start.25 = (bf16[128,24]{0,1:T(8,128)(2,1)S(1)}, bf16[128,24]{0,1:T(8,128)(2,1)}, u32[]{:S(2)}) copy-start(bf16[128,24]{0,1:T(8,128)(2,1)} %get-tuple-element.176) | copy-start | bytes 18436
  38.0 14.1 %copy-start.26 = (bf16[128,24]{0,1:T(8,128)(2,1)S(1)}, bf16[128,24]{0,1:T(8,128)(2,1)}, u32[]{:S(2)}) copy-start(bf16[128,24]{0,1:T(8,128)(2,1)} %get-tuple-element.177) | copy-start | bytes 18436
  38.0 16.4 %copy-start.3 = (bf16[1,128,128]{2,0,1:T(2,128)(2,1)S(1)}, bf16[1,128,128]{2,0,1:T(2,128)(2,1)}, u32[]{:S(2)}) copy-start(bf16[1,128,128]{2,0,1:T(2,128)(2,1)} %get-tuple-element.175) | copy-start | bytes 98308
  42.0 12.3 %copy-start.32 = (s32[128]{0:T(128)S(1)}, s32[128]{0:T(128)}, u32[]{:S(2)}) copy-start(s32[128]{0:T(128)} %get-tuple-element.183) | copy-start | bytes 1540
  42.0 12.3 %copy-start.33 = (s32[128]{0:T(128)S(1)}, s32[128]{0:T(128)}, u32[]{:S(2)}) copy-start(s32[128]{0:T(128)} %get-tuple-element.184) | copy-start | bytes 1540
  42.0 12.5 %copy-start.10 = (bf16[1,1,1,2,128,16]{4,5,3,2,1,0:T(8,128)(2,1)S(1)}, bf16[1,1,1,2,128,16]{4,5,3,2,1,0:T(8,128)(2,1)}, u32[]{:S(2)}) copy-start(bf16[1,1,1,2,128,16]{4,5,3,2,1,0:T(8,128)(2,1)} %get-tuple-element.153) | copy-start | bytes 24580
  42.0 12.6 %copy-start.6 = (s32[128,128]{1,0:T(8,128)S(1)}, s32[128,128]{1,0:T(8,128)}, u32[]{:S(2)}) copy-start(s32[128,128]{1,0:T(8,128)} %get-tuple-element.205) | copy-start | bytes 196612
  43.0 24.5 %copy-start.15 = (bf16[128,128]{1,0:T(8,128)(2,1)S(1)}, bf16[128,128]{1,0:T(8,128)(2,1)}, u32[]{:S(2)}) copy-start(bf16[128,128]{1,0:T(8,128)(2,1)} %get-tuple-element.126) | copy-start | bytes 98308
  43.0 24.5 %copy-start.16 = (bf16[128,128]{1,0:T(8,128)(2,1)S(1)}, bf16[128,128]{1,0:T(8,128)(2,1)}, u32[]{:S(2)}) copy-start(bf16[128,128]{1,0:T(8,128)(2,1)} %get-tuple-element.127) | copy-start | bytes 98308
  43.0 24.5 %copy-start.21 = (bf16[128,128]{1,0:T(8,128)(2,1)S(1)}, bf16[128,128]{1,0:T(8,128)(2,1)}, u32[]{:S(2)}) copy-start(bf16[128,128]{1,0:T(8,128)(2,1)} %get-tuple-element.128) | copy-start | bytes 98308
  43.0 24.5 %copy-start.22 = (bf16[128,128]{1,0:T(8,128)(2,1)S(1)}, bf16[128,128]{1,0:T(8,128)(2,1)}, u32[]{:S(2)}) copy-start(bf16[128,128]{1,0:T(8,128)(2,1)} %get-tuple-element.129) | copy-start | bytes 98308
  43.0 8.6 %all-to-all-start = ((bf16[4,2,6,1024]{3,1,2,0:T(2,128)(2,1)}), bf16[4,2,6,1024]{3,1,2,0:T(2,128)(2,1)S(1)}, u32[]{:S(2)}, u32[]{:S(2)}) async-start(bf16[4,2,6,1024]{3,1,2,0:T(2,128)(2,1)} %pad_maximum_fusion), calls=%async_computation | async-start | bytes 196608 | tf_op jit(solution)/shard_map/all_to_all | solution.py:107
  52.4 15.0 %collective-permute-start.1 = (bf16[2,128,1024]{2,1,0:T(8,128)(2,1)S(1)}, bf16[2,128,1024]{2,1,0:T(8,128)(2,1)S(1)}, u32[]{:S(2)}, u32[]{:S(2)}) collective-permute-start(bf16[2,128,1024]{2,1,0:T(8,128)(2,1)S(1)} %bitcast.240), channel_id=1, source_target_pairs={{0,4},{4,0},{8,12},{12,8},{16,20},{20,16},{24,28},{28,24},{32,36},... | collective-permute-start | bytes 1572872 | tf_op jit(solution)/shard_map/ppermute | solution.py:22
  68.0 28.0 %copy-start.13 = (bf16[128,128]{1,0:T(8,128)(2,1)S(1)}, bf16[128,128]{1,0:T(8,128)(2,1)}, u32[]{:S(2)}) copy-start(bf16[128,128]{1,0:T(8,128)(2,1)} %get-tuple-element.122) | copy-start | bytes 98308
  68.0 28.0 %copy-start.14 = (bf16[128,128]{1,0:T(8,128)(2,1)S(1)}, bf16[128,128]{1,0:T(8,128)(2,1)}, u32[]{:S(2)}) copy-start(bf16[128,128]{1,0:T(8,128)(2,1)} %get-tuple-element.123) | copy-start | bytes 98308
  68.0 28.0 %copy-start.19 = (bf16[128,128]{1,0:T(8,128)(2,1)S(1)}, bf16[128,128]{1,0:T(8,128)(2,1)}, u32[]{:S(2)}) copy-start(bf16[128,128]{1,0:T(8,128)(2,1)} %get-tuple-element.124) | copy-start | bytes 98308
  68.0 28.0 %copy-start.20 = (bf16[128,128]{1,0:T(8,128)(2,1)S(1)}, bf16[128,128]{1,0:T(8,128)(2,1)}, u32[]{:S(2)}) copy-start(bf16[128,128]{1,0:T(8,128)(2,1)} %get-tuple-element.125) | copy-start | bytes 98308
  68.0 28.0 %collective-permute-start.2 = (bf16[2,128,1024]{2,1,0:T(8,128)(2,1)S(1)}, bf16[2,128,1024]{2,1,0:T(8,128)(2,1)S(1)}, u32[]{:S(2)}, u32[]{:S(2)}) collective-permute-start(bf16[2,128,1024]{2,1,0:T(8,128)(2,1)S(1)} %bitcast.253), channel_id=1, source_target_pairs={{0,8},{8,0},{4,12},{12,4},{16,24},{24,16},{20,28},{28,20},{32,40},... | collective-permute-start | bytes 1572872 | tf_op jit(solution)/shard_map/ppermute | solution.py:22
  96.0 3.5 %copy-start.29 = (s32[128]{0:T(128)S(1)}, s32[128]{0:T(128)}, u32[]{:S(2)}) copy-start(s32[128]{0:T(128)} %get-tuple-element.185) | copy-start | bytes 1540
  96.0 3.6 %copy-start.1 = (bf16[1,128,128]{2,0,1:T(2,128)(2,1)S(1)}, bf16[1,128,128]{2,0,1:T(2,128)(2,1)}, u32[]{:S(2)}) copy-start(bf16[1,128,128]{2,0,1:T(2,128)(2,1)} %get-tuple-element.167) | copy-start | bytes 98308
  96.1 3.6 %copy-start.8 = (bf16[1,1,1,2,128,16]{4,5,3,2,1,0:T(8,128)(2,1)S(1)}, bf16[1,1,1,2,128,16]{4,5,3,2,1,0:T(8,128)(2,1)}, u32[]{:S(2)}) copy-start(bf16[1,1,1,2,128,16]{4,5,3,2,1,0:T(8,128)(2,1)} %get-tuple-element.146) | copy-start | bytes 24580
  96.5 28.7 %copy-start.11 = (bf16[128,128]{1,0:T(8,128)(2,1)S(1)}, bf16[128,128]{1,0:T(8,128)(2,1)}, u32[]{:S(2)}) copy-start(bf16[128,128]{1,0:T(8,128)(2,1)} %get-tuple-element.118) | copy-start | bytes 98308
  96.5 28.7 %copy-start.12 = (bf16[128,128]{1,0:T(8,128)(2,1)S(1)}, bf16[128,128]{1,0:T(8,128)(2,1)}, u32[]{:S(2)}) copy-start(bf16[128,128]{1,0:T(8,128)(2,1)} %get-tuple-element.119) | copy-start | bytes 98308
  96.5 28.7 %copy-start.17 = (bf16[128,128]{1,0:T(8,128)(2,1)S(1)}, bf16[128,128]{1,0:T(8,128)(2,1)}, u32[]{:S(2)}) copy-start(bf16[128,128]{1,0:T(8,128)(2,1)} %get-tuple-element.120) | copy-start | bytes 98308
  96.6 28.7 %copy-start.18 = (bf16[128,128]{1,0:T(8,128)(2,1)S(1)}, bf16[128,128]{1,0:T(8,128)(2,1)}, u32[]{:S(2)}) copy-start(bf16[128,128]{1,0:T(8,128)(2,1)} %get-tuple-element.121) | copy-start | bytes 98308
  96.6 28.6 %collective-permute-start.3 = (bf16[2,128,1024]{2,1,0:T(8,128)(2,1)S(1)}, bf16[2,128,1024]{2,1,0:T(8,128)(2,1)S(1)}, u32[]{:S(2)}, u32[]{:S(2)}) collective-permute-start(bf16[2,128,1024]{2,1,0:T(8,128)(2,1)S(1)} %bitcast.254), channel_id=1, source_target_pairs={{0,16},{16,0},{4,20},{20,4},{8,24},{24,8},{12,28},{28,12},{32,48},... | collective-permute-start | bytes 1572872 | tf_op jit(solution)/shard_map/ppermute | solution.py:22
  125.8 14.6 %collective-permute-start.4 = (bf16[2,128,1024]{2,1,0:T(8,128)(2,1)S(1)}, bf16[2,128,1024]{2,1,0:T(8,128)(2,1)S(1)}, u32[]{:S(2)}, u32[]{:S(2)}) collective-permute-start(bf16[2,128,1024]{2,1,0:T(8,128)(2,1)S(1)} %bitcast.255), channel_id=1, source_target_pairs={{0,32},{32,0},{4,36},{36,4},{8,40},{40,8},{12,44},{44,12},{16,48},... | collective-permute-start | bytes 1572872 | tf_op jit(solution)/shard_map/ppermute | solution.py:22
  140.8 27.8 %collective-permute-start.5 = (bf16[2,128,1024]{2,1,0:T(8,128)(2,1)S(1)}, bf16[2,128,1024]{2,1,0:T(8,128)(2,1)S(1)}, u32[]{:S(2)}, u32[]{:S(2)}) collective-permute-start(bf16[2,128,1024]{2,1,0:T(8,128)(2,1)S(1)} %bitcast.256), channel_id=1, source_target_pairs={{0,64},{64,0},{4,68},{68,4},{8,72},{72,8},{12,76},{76,12},{16,80},... | collective-permute-start | bytes 1572872 | tf_op jit(solution)/shard_map/ppermute | solution.py:22
  (10 other events, 24.0 us)
